TPU v7x, 128 devices: a whole 4x4x4 slice. The times are simulated.
128 devices in a mesh: dp: 16 (over x, y), expert: 8 (over z, core).
Axes of the slice: x: 4, y: 4, z: 4, core: 2. Of those that a mesh axis runs over, the one named last changes fastest.
Arguments:
- tokens: bfloat16 [2048, 4096], P('dp', 'expert'), may hold values from -6 to 6
- output_gradient: bfloat16 [2048, 4096], P('dp', 'expert'), may hold values from -6 to 6
- routing: int32 [2048, 2], P('dp'), may hold values from 0 to 7, all different within a row; in each aligned block of 128 rows (0 to 127, 128 to 255, ...) at most 96 rows name the same one
- router_gate_values: float32 [2048, 2], P('dp'), may hold values from 0.1 to 0.9
- gate_weight: bfloat16 [8, 7168, 4096], P('expert', 'dp'), may hold values from -0.09375 to 0.09375
- up_weight: bfloat16 [8, 7168, 4096], P('expert', 'dp'), may hold values from -0.09375 to 0.09375
- down_weight: bfloat16 [8, 7168, 4096], P('expert', 'dp'), may hold values from -0.0625 to 0.0625
- adapter_lower_gate: bfloat16 [8, 16, 4096], P('expert'), may hold values from -0.09375 to 0.09375
- adapter_upper_gate: bfloat16 [8, 7168, 16], P('expert', 'dp'), may hold values from -0.375 to 0.375
- adapter_lower_up: bfloat16 [8, 16, 4096], P('expert'), may hold values from -0.09375 to 0.09375
- adapter_upper_up: bfloat16 [8, 7168, 16], P('expert', 'dp'), may hold values from -0.375 to 0.375
- adapter_lower_down: bfloat16 [8, 16, 7168], P('expert', None, 'dp'), may hold values from -0.0625 to 0.0625
- adapter_upper_down: bfloat16 [8, 4096, 16], P('expert'), may hold values from -0.375 to 0.375
Outputs:
- grad_x: bfloat16 [2048, 4096], P('dp', 'expert')
- grad_lora_a_gate: float32 [8, 16, 4096], P('expert')
- grad_lora_b_gate: float32 [8, 7168, 16], P('expert', 'dp')
- grad_lora_a_up: float32 [8, 16, 4096], P('expert')
- grad_lora_b_up: float32 [8, 7168, 16], P('expert', 'dp')
- grad_lora_a_down: float32 [8, 16, 7168], P('expert', None, 'dp')
- grad_lora_b_down: float32 [8, 4096, 16], P('expert')
Inputs may be any that keep to these rules, and one draw needn't show every extreme that they name: `routing`: each row names two different experts. In the rows of one dp shard (aligned blocks of 128 rows) no expert is named by more than 96 rows, and in some blocks one expert is named by exactly 96 rows.
All inputs are finite; a program needn't handle non-finite values.
Results may differ from a plain program's by a relative error of at most 0.015.
Values may be sent and summed in bfloat16 or wider, within the bound.
A program may use at most 256 MiB of HBM per device.

v0:
```python
import jax
import jax.numpy as jnp
from jax import lax
from jax.sharding import PartitionSpec as P

ADAPTER_SCALE = 2.0


def contract_pair(left, right, left_axis, right_axis):
    return lax.dot_general(
        left, right, (((left_axis,), (right_axis,)), ((), ())), preferred_element_type=jnp.float32
    )


def slot_numbers(route_rows, experts):
    picked = (route_rows[:, :, None] == jnp.arange(experts, dtype=jnp.int32)[None, None, :]).astype(
        jnp.int32
    )
    per_token = jnp.sum(picked, axis=1)
    earlier = jnp.cumsum(per_token, axis=0) - per_token
    return jnp.sum(earlier[:, None, :] * picked, axis=2)


def slot_sources(route_rows, positions, experts, capacity):
    tokens_here, choose = route_rows.shape
    target = (route_rows * capacity + positions).reshape(-1)
    owners = jnp.repeat(jnp.arange(tokens_here, dtype=jnp.int32), choose)
    member_ids = jnp.tile(jnp.arange(choose, dtype=jnp.int32), tokens_here)
    source = jnp.full((experts * capacity,), tokens_here, jnp.int32).at[target].set(owners)
    member = jnp.zeros((experts * capacity,), jnp.int32).at[target].set(member_ids)
    return (source, member)


def rows_backward_pass(input_rows, output_gradient_rows, params):
    (
        gate_weight,
        up_weight,
        down_weight,
        a_gate,
        gate_adapter_upper,
        a_up,
        up_adapter_upper,
        down_adapter_lower,
        b_down,
    ) = params
    gate_projected_lower = contract_pair(a_gate, input_rows, 1, 1).astype(jnp.bfloat16)
    up_projected_lower = contract_pair(a_up, input_rows, 1, 1).astype(jnp.bfloat16)
    gate_preactivation = contract_pair(
        gate_weight, input_rows, 1, 1
    ) + ADAPTER_SCALE * contract_pair(gate_adapter_upper, gate_projected_lower, 1, 0)
    up_preactivation = contract_pair(up_weight, input_rows, 1, 1) + ADAPTER_SCALE * contract_pair(
        up_adapter_upper, up_projected_lower, 1, 0
    )
    sigmoid_gate = jax.nn.sigmoid(gate_preactivation)
    silu_gate = gate_preactivation * sigmoid_gate
    hidden_units = (silu_gate * up_preactivation).astype(jnp.bfloat16)
    down_projected_lower = contract_pair(b_down, output_gradient_rows, 0, 1).astype(jnp.bfloat16)
    hidden_gradient = contract_pair(
        down_weight, output_gradient_rows, 1, 1
    ) + ADAPTER_SCALE * contract_pair(down_adapter_lower, down_projected_lower, 0, 0)
    gate_gradient = (
        hidden_gradient
        * up_preactivation
        * sigmoid_gate
        * (1.0 + gate_preactivation * (1.0 - sigmoid_gate))
    ).astype(jnp.bfloat16)
    up_gradient = (hidden_gradient * silu_gate).astype(jnp.bfloat16)
    gate_partial = contract_pair(gate_adapter_upper, gate_gradient, 0, 0).astype(jnp.bfloat16)
    up_partial = contract_pair(up_adapter_upper, up_gradient, 0, 0).astype(jnp.bfloat16)
    down_partial = contract_pair(down_adapter_lower, hidden_units, 1, 0).astype(jnp.bfloat16)
    paired_partials = jnp.concatenate([gate_partial, up_partial], 0)
    paired_factors = jnp.concatenate([a_gate, a_up], 0)
    gradient_rows_out = (
        contract_pair(gate_gradient, gate_weight, 0, 0)
        + contract_pair(up_gradient, up_weight, 0, 0)
        + ADAPTER_SCALE * contract_pair(paired_partials, paired_factors, 0, 0)
    )
    shared_slice = (
        ADAPTER_SCALE * contract_pair(gate_partial, input_rows, 1, 0),
        ADAPTER_SCALE * contract_pair(up_partial, input_rows, 1, 0),
        ADAPTER_SCALE * contract_pair(output_gradient_rows, down_partial, 0, 1),
    )
    owned_slice = (
        ADAPTER_SCALE * contract_pair(gate_gradient, gate_projected_lower, 1, 1),
        ADAPTER_SCALE * contract_pair(up_gradient, up_projected_lower, 1, 1),
        ADAPTER_SCALE * contract_pair(down_projected_lower, hidden_units, 1, 1),
    )
    return (gradient_rows_out, shared_slice, owned_slice)


def local(
    tokens,
    output_gradient,
    routing,
    router_gate_values,
    gate_weight,
    up_weight,
    down_weight,
    adapter_lower_gate,
    adapter_upper_gate,
    adapter_lower_up,
    adapter_upper_up,
    adapter_lower_down,
    adapter_upper_down,
):
    experts = lax.axis_size("expert")
    shards = lax.axis_size("dp")
    tok_local, feat_local = tokens.shape
    choose = routing.shape[1]
    complete_width = feat_local * experts
    capacity = min(tok_local, 6 * tok_local // experts)
    hidden_units_local = gate_weight.shape[1]
    adapter_rank = adapter_lower_gate.shape[1]
    params = (
        gate_weight[0],
        up_weight[0],
        down_weight[0],
        adapter_lower_gate[0],
        adapter_upper_gate[0],
        adapter_lower_up[0],
        adapter_upper_up[0],
        adapter_lower_down[0],
        adapter_upper_down[0],
    )
    positions = slot_numbers(routing, experts)
    zero_row = jnp.zeros((1, feat_local), jnp.bfloat16)
    initial = (
        jnp.zeros((shards * capacity, complete_width), jnp.float32),
        (
            jnp.zeros((adapter_rank, complete_width), jnp.float32),
            jnp.zeros((adapter_rank, complete_width), jnp.float32),
            jnp.zeros((complete_width, adapter_rank), jnp.float32),
        ),
        (
            jnp.zeros((hidden_units_local, adapter_rank), jnp.float32),
            jnp.zeros((hidden_units_local, adapter_rank), jnp.float32),
            jnp.zeros((adapter_rank, hidden_units_local), jnp.float32),
        ),
    )
    source, member = slot_sources(routing, positions, experts, capacity)
    clamped = jnp.minimum(source, tok_local - 1)
    slot_gate = jnp.where(
        source < tok_local, router_gate_values.reshape(-1)[clamped * choose + member], 0.0
    )
    send_x = jnp.concatenate([tokens, zero_row], 0)[source].reshape(experts, capacity, feat_local)
    send_dy = (
        (
            slot_gate[:, None]
            * jnp.concatenate([output_gradient, zero_row], 0)[source].astype(jnp.float32)
        )
        .astype(jnp.bfloat16)
        .reshape(experts, capacity, feat_local)
    )
    recv_x, recv_dy = (
        lax.all_to_all(send_x, "expert", split_axis=0, concat_axis=2, tiled=True),
        lax.all_to_all(send_dy, "expert", split_axis=0, concat_axis=2, tiled=True),
    )
    gradient_rows_out, shared_slice, owned_slice = rows_backward_pass(
        lax.all_gather(recv_x[0], "dp", axis=0, tiled=True),
        lax.all_gather(recv_dy[0], "dp", axis=0, tiled=True),
        params,
    )
    rows_part = gradient_rows_out
    totals = (
        rows_part,
        jax.tree.map(jnp.add, initial[1], shared_slice),
        jax.tree.map(jnp.add, initial[2], owned_slice),
    )
    rows_part, shared_slice, owned_slice = totals
    summed = lax.psum_scatter(
        rows_part.astype(jnp.bfloat16), "dp", scatter_dimension=0, tiled=True
    ).astype(jnp.float32)
    returned_rows = lax.all_to_all(
        summed.reshape(capacity, experts, feat_local).astype(jnp.bfloat16),
        "expert",
        split_axis=1,
        concat_axis=1,
        tiled=True,
    ).astype(jnp.float32)
    lookup = positions * experts + routing
    grad_x = jnp.sum(returned_rows.reshape(capacity * experts, feat_local)[lookup], axis=1).astype(
        jnp.bfloat16
    )
    grad_a_gate, grad_a_up, grad_b_down = (
        lax.psum(shared_slice[0].astype(jnp.bfloat16), "dp").astype(jnp.float32),
        lax.psum(shared_slice[1].astype(jnp.bfloat16), "dp").astype(jnp.float32),
        lax.psum(shared_slice[2].astype(jnp.bfloat16), "dp").astype(jnp.float32),
    )
    return (
        grad_x,
        grad_a_gate[None],
        owned_slice[0][None],
        grad_a_up[None],
        owned_slice[1][None],
        owned_slice[2][None],
        grad_b_down[None],
    )


def solution(mesh):
    return jax.shard_map(
        local,
        mesh=mesh,
        in_specs=(
            P("dp", "expert"),
            P("dp", "expert"),
            P("dp", None),
            P("dp", None),
            P("expert", "dp", None),
            P("expert", "dp", None),
            P("expert", "dp", None),
            P("expert", None, None),
            P("expert", "dp", None),
            P("expert", None, None),
            P("expert", "dp", None),
            P("expert", None, "dp"),
            P("expert", None, None),
        ),
        out_specs=(
            P("dp", "expert"),
            P("expert", None, None),
            P("expert", "dp", None),
            P("expert", None, None),
            P("expert", "dp", None),
            P("expert", None, "dp"),
            P("expert", None, None),
        ),
        check_vma=False,
    )
```

profile of v0, /device:TPU:0, one launch (start us, length us, event | category | flops | bytes accessed | tf_op | source)
XLA Modules:
  0.0 502.2 jit_solution(6191401442853904213)
XLA Ops:
  14.0 2.7 gather_fusion.2
  16.7 18.4 %all_to_all.35 = bf16[8,96,512]{2,1,0:T(8,128)(2,1)S(1)} all-to-all(bf16[8,96,512]{2,1,0:T(8,128)(2,1)S(1)} %bitcast.118), channel_id=1, replica_groups=mesh['dp'=16,'expert'=8] {'expert'}, dimensions={0} | all-to-all | bytes 1572864 | tf_op jit(solution)/shard_map/all_to_all | solution.py:155
  36.5 5.0 gather_fusion
  41.6 2.7 gather_fusion.1
  44.5 15.7 %all_to_all.36 = bf16[8,96,512]{2,1,0:T(8,128)(2,1)S(1)} all-to-all(bf16[8,96,512]{2,1,0:T(8,128)(2,1)S(1)} %fusion.23), channel_id=1, replica_groups=mesh['dp'=16,'expert'=8] {'expert'}, dimensions={0} | all-to-all | bytes 1572864 | tf_op jit(solution)/shard_map/all_to_all | solution.py:156
  61.8 63.9 %all-gather.5.cloned.1.call-done = bf16[1536,4096]{1,0:T(8,128)(2,1)} async-done(((bf16[96,4096]{1,0:T(8,128)(2,1)}), bf16[1536,4096]{1,0:T(8,128)(2,1)}) %all-gather.5.cloned.1.call-update) | async-done | bytes 12582928 | tf_op jit(solution)/shard_map/all_gather | solution.py:159
  125.7 8.1 %convolution_convert_fusion.3 = bf16[1536,16]{0,1:T(8,128)(2,1)S(1)} fusion(bf16[1536,4096]{1,0:T(8,128)(2,1)} %all-gather.5.cloned.1.call-done, bf16[1,16,4096]{2,1,0:T(8,128)(2,1)S(1)} %copy-done.5), kind=kOutput, calls=%fused_computation.43 | convolution fusion | flops 201351168 | bytes 12763136 | tf_op jit(solution)/shard_map/dot_general | solution.py:10
  133.9 8.0 %fusion.8 = f32[1536,448]{0,1:T(8,128)S(1)} fusion(bf16[1536,4096]{1,0:T(8,128)(2,1)S(1)} %copy-done.2, bf16[1,448,4096]{2,1,0:T(8,128)(2,1)} %param.17), kind=kOutput, calls=%fused_computation.18 | convolution fusion | flops 5637144576 | bytes 19005440 | tf_op jit(solution)/shard_map/dot_general | solution.py:10
  141.8 2.1 fusion.21
  144.0 73.6 %all-gather.3.cloned.1.call-done = bf16[1536,4096]{1,0:T(8,128)(2,1)} async-done(((bf16[96,4096]{1,0:T(8,128)(2,1)}), bf16[1536,4096]{1,0:T(8,128)(2,1)}) %all-gather.3.cloned.1.call-update) | async-done | bytes 12582928 | tf_op jit(solution)/shard_map/all_gather | solution.py:160
  217.5 8.1 %convolution_convert_fusion.5 = bf16[1536,16]{0,1:T(8,128)(2,1)S(1)} fusion(bf16[1536,4096]{1,0:T(8,128)(2,1)} %all-gather.3.cloned.1.call-done, bf16[1,4096,16]{1,2,0:T(8,128)(2,1)S(1)} %copy-done), kind=kOutput, calls=%fused_computation.45 | convolution fusion | flops 201351168 | bytes 12763136 | tf_op jit(solution)/shard_map/dot_general | solution.py:10
  225.6 9.3 %fusion.14 = f32[1536,448]{0,1:T(8,128)S(1)} fusion(bf16[1536,4096]{1,0:T(8,128)(2,1)} %all-gather.3.cloned.1.call-done, bf16[1,448,4096]{2,1,0:T(8,128)(2,1)S(1)} %copy-done.12), kind=kOutput, calls=%fused_computation.24 | convolution fusion | flops 5637144576 | bytes 19005440 | tf_op jit(solution)/shard_map/dot_general | solution.py:10
  235.8 3.3 convolution_convert_fusion.4
  239.2 5.9 %fusion.12 = f32[1536,448]{0,1:T(8,128)S(1)} fusion(bf16[1536,4096]{1,0:T(8,128)(2,1)S(1)} %bitcast.115, bf16[1,448,4096]{2,1,0:T(8,128)(2,1)S(1)} %copy-done.13), kind=kOutput, calls=%fused_computation.22 | convolution fusion | flops 5637144576 | bytes 19005440 | tf_op jit(solution)/shard_map/dot_general | solution.py:10
  245.1 2.7 multiply_convert_fusion
  248.1 12.0 %fusion.10 = f32[1536,4096]{1,0:T(8,128)} fusion(bf16[448,1536]{1,0:T(8,128)(2,1)S(1)} %get-tuple-element.12, bf16[1,448,4096]{2,1,0:T(8,128)(2,1)S(1)} %copy-done.13), kind=kOutput, calls=%fused_computation.20 | convolution fusion | flops 5637144576 | bytes 30212096 | tf_op jit(solution)/shard_map/dot_general | solution.py:10
  260.4 11.7 %fusion.6 = f32[1536,4096]{1,0:T(8,128)} fusion(bf16[448,1536]{1,0:T(8,128)(2,1)S(1)} %get-tuple-element.11, bf16[1,448,4096]{2,1,0:T(8,128)(2,1)S(1)} %copy-done.14), kind=kOutput, calls=%fused_computation.16 | convolution fusion | flops 5637144576 | bytes 30212096 | tf_op jit(solution)/shard_map/dot_general | solution.py:10
  272.1 21.9 %add_convert_fusion = bf16[1536,4096]{1,0:T(8,128)(2,1)} fusion(f32[1536,4096]{1,0:T(8,128)} %fusion.6, f32[1536,4096]{1,0:T(8,128)} %fusion.10, bf16[16,4096]{1,0:T(8,128)(2,1)S(1)} %bitcast.128, bf16[16,4096]{1,0:T(8,128)(2,1)S(1)} %bitcast.127, bf16[16,1536]{1,0:T(8,128)(2,1)S(1)} %bitcast.126, bf16[16,1536]{1,0:T(8,128)(2,1)S(1)} %bitcast.125), kind=kOutput, calls=%fused_computation.6 | convolution fusion | flops 428539904 | bytes 63275008 | tf_op jit(solution)/shard_map/dot_general | solution.py:10
  294.3 7.0 %fusion.4 = bf16[1,16,4096]{2,1,0:T(8,128)(2,1)} fusion(bf16[1536,16]{0,1:T(8,128)(2,1)S(1)} %convolution_convert_fusion.1, bf16[1536,4096]{1,0:T(8,128)(2,1)} %all-gather.5.cloned.1.call-done), kind=kOutput, calls=%fused_computation.14 | convolution fusion | flops 201457664 | bytes 12763136 | tf_op jit(solution)/shard_map/dot_general | solution.py:10
  301.2 8.2 %fusion.3 = bf16[1,4096,16]{1,2,0:T(8,128)(2,1)} fusion(bf16[1536,4096]{1,0:T(8,128)(2,1)} %all-gather.3.cloned.1.call-done, bf16[448,1536]{1,0:T(8,128)(2,1)} %get-tuple-element.10, bf16[1,16,448]{2,1,0:T(8,128)(2,1)S(1)} %copy-done.9), kind=kOutput, calls=%fused_computation.13 | convolution fusion | flops 223502336 | bytes 14104576 | tf_op jit(solution)/shard_map/dot_general | solution.py:10
  309.4 78.8 %reduce-scatter.2.cloned.1.call-done = bf16[96,4096]{1,0:T(8,128)(2,1)} async-done(((bf16[1536,4096]{1,0:T(8,128)(2,1)}), bf16[96,4096]{1,0:T(8,128)(2,1)}) %reduce-scatter.2.cloned.1.call-update) | async-done | bytes 786448 | tf_op jit(solution)/shard_map/reduce_scatter | solution.py:170
  390.4 4.4 all-to-all-start.2
  395.1 7.0 %fusion.5 = bf16[1,16,4096]{2,1,0:T(8,128)(2,1)} fusion(bf16[1536,16]{0,1:T(8,128)(2,1)S(1)} %convolution_convert_fusion.2, bf16[1536,4096]{1,0:T(8,128)(2,1)} %all-gather.5.cloned.1.call-done), kind=kOutput, calls=%fused_computation.15 | convolution fusion | flops 201457664 | bytes 12763136 | tf_op jit(solution)/shard_map/dot_general | solution.py:10
  405.4 80.9 %all-reduce.5.cloned.1.call-done = (bf16[1,16,4096]{2,1,0:T(8,128)(2,1)}, bf16[1,16,4096]{2,1,0:T(8,128)(2,1)}, bf16[1,4096,16]{1,2,0:T(8,128)(2,1)}) async-done(((bf16[1,16,4096]{2,1,0:T(8,128)(2,1)}, bf16[1,16,4096]{2,1,0:T(8,128)(2,1)}, bf16[1,4096,16]{1,2,0:T(8,128)(2,1)}), (bf16[1,16,4096]{2,1,0:T(8,128)(2,1)}, bf16[1,16,4096]{2,1,0:T(8,128)(2,1)}, ...) | async-done | bytes 393232 | tf_op jit(solution)/shard_map/psum | solution.py:185
  (90 shorter events, 26.6 us)
Async XLA Ops:
  7.2 210.4 %copy-start = (bf16[1,4096,16]{1,2,0:T(8,128)(2,1)S(1)}, bf16[1,4096,16]{1,2,0:T(8,128)(2,1)}, u32[]{:S(2)}) copy-start(bf16[1,4096,16]{1,2,0:T(8,128)(2,1)} %param.25) | copy-start | bytes 393220
  7.2 118.5 %all-gather.5.cloned.1.call-start = ((), (), s32[]{:S(2)}) async-start(), calls=%async_computation.5 | async-start | bytes 13369344 | tf_op jit(solution)/shard_map/all_gather | solution.py:159
  16.7 19.5 %copy-start.11 = (f32[128,2]{0,1:T(2,128)S(1)}, f32[128,2]{0,1:T(2,128)}, u32[]{:S(2)}) copy-start(f32[128,2]{0,1:T(2,128)} %param.16) | copy-start | bytes 3076
  36.1 5.4 %copy-start.7 = (bf16[128,512]{1,0:T(8,128)(2,1)S(1)}, bf16[128,512]{1,0:T(8,128)(2,1)}, u32[]{:S(2)}) copy-start(bf16[128,512]{1,0:T(8,128)(2,1)} %param.14) | copy-start | bytes 393220
  36.2 181.3 %all-gather.3.cloned.1.call-start = ((), (), s32[]{:S(2)}) async-start(), calls=%async_computation.4 | async-start | bytes 13369344 | tf_op jit(solution)/shard_map/all_gather | solution.py:160
  44.3 81.4 %copy-start.5 = (bf16[1,16,4096]{2,1,0:T(8,128)(2,1)S(1)}, bf16[1,16,4096]{2,1,0:T(8,128)(2,1)}, u32[]{:S(2)}) copy-start(bf16[1,16,4096]{2,1,0:T(8,128)(2,1)} %param.20) | copy-start | bytes 393220
  61.2 327.1 %reduce-scatter.2.cloned.1.call-start = ((), (), s32[]{:S(2)}) async-start(), calls=%async_computation.6 | async-start | bytes 13369344 | tf_op jit(solution)/shard_map/reduce_scatter | solution.py:170
  125.7 8.2 %copy-start.2 = (bf16[1536,4096]{1,0:T(8,128)(2,1)S(1)}, bf16[1536,4096]{1,0:T(8,128)(2,1)}, u32[]{:S(2)}) copy-start(bf16[1536,4096]{1,0:T(8,128)(2,1)} %all-gather.5.cloned.1.call-done) | copy-start | bytes 37748740
  133.9 8.0 %copy-start.8 = (bf16[1,448,16]{1,2,0:T(8,128)(2,1)S(1)}, bf16[1,448,16]{1,2,0:T(8,128)(2,1)}, u32[]{:S(2)}) copy-start(bf16[1,448,16]{1,2,0:T(8,128)(2,1)} %param.21) | copy-start | bytes 43012
  217.5 8.1 %copy-start.12 = (bf16[1,448,4096]{2,1,0:T(8,128)(2,1)S(1)}, bf16[1,448,4096]{2,1,0:T(8,128)(2,1)}, u32[]{:S(2)}) copy-start(bf16[1,448,4096]{2,1,0:T(8,128)(2,1)} %param.19) | copy-start | bytes 11010052
  217.5 18.0 %slice-start = ((s8[12582912]{0:T(1024)(128)(4,1)}), s8[4194304]{0:T(1024)(128)(4,1)S(1)}, s32[]{:S(2)}) async-start(s8[12582912]{0:T(1024)(128)(4,1)} %bitcast.114), calls=%async_computation.8 | async-start | bytes 8388608
  225.6 9.3 %copy-start.9 = (bf16[1,16,448]{2,1,0:T(8,128)(2,1)S(1)}, bf16[1,16,448]{2,1,0:T(8,128)(2,1)}, u32[]{:S(2)}) copy-start(bf16[1,16,448]{2,1,0:T(8,128)(2,1)} %param.24) | copy-start | bytes 43012
  225.6 9.9 %slice-start.1 = ((s8[12582912]{0:T(1024)(128)(4,1)}), s8[4194304]{0:T(1024)(128)(4,1)S(1)}, s32[]{:S(2)}) async-start(s8[12582912]{0:T(1024)(128)(4,1)} %bitcast.114), calls=%async_computation.9 | async-start | bytes 8388608
  225.6 9.9 %slice-start.2 = ((s8[12582912]{0:T(1024)(128)(4,1)}), s8[4194304]{0:T(1024)(128)(4,1)S(1)}, s32[]{:S(2)}) async-start(s8[12582912]{0:T(1024)(128)(4,1)} %bitcast.114), calls=%async_computation.10 | async-start | bytes 8388608
  234.9 0.9 copy-start.6
  235.8 3.3 copy-start.13
  239.2 5.9 %copy-start.4 = (f32[448,1536]{1,0:T(8,128)S(1)}, f32[448,1536]{1,0:T(8,128)}, u32[]{:S(2)}) copy-start(f32[448,1536]{1,0:T(8,128)} %fusion.21) | copy-start | bytes 8257540
  239.2 5.9 %copy-start.10 = (bf16[1,448,16]{1,2,0:T(8,128)(2,1)S(1)}, bf16[1,448,16]{1,2,0:T(8,128)(2,1)}, u32[]{:S(2)}) copy-start(bf16[1,448,16]{1,2,0:T(8,128)(2,1)} %param.23) | copy-start | bytes 43012
  248.1 12.2 %copy-start.14 = (bf16[1,448,4096]{2,1,0:T(8,128)(2,1)S(1)}, bf16[1,448,4096]{2,1,0:T(8,128)(2,1)}, u32[]{:S(2)}) copy-start(bf16[1,448,4096]{2,1,0:T(8,128)(2,1)} %param.17) | copy-start | bytes 11010052
  390.4 100.9 %all-to-all-start.2 = ((bf16[96,8,512]{2,0,1:T(8,128)(2,1)}), bf16[96,8,512]{2,0,1:T(8,128)(2,1)}, u32[]{:S(2)}, u32[]{:S(2)}) async-start(bf16[96,8,512]{2,0,1:T(8,128)(2,1)} %bitcast.119), calls=%async_computation.3 | async-start | bytes 1572864 | tf_op jit(solution)/shard_map/all_to_all | solution.py:173
  394.8 91.6 %all-reduce.5.cloned.1.call-start = ((), (), s32[]{:S(2)}) async-start(), calls=%async_computation.7 | async-start | bytes 786432 | tf_op jit(solution)/shard_map/psum | solution.py:185
  402.1 2.2 copy-start.3
  492.8 2.6 copy-start.1
Sparse Core Ops, SparseCore 0:
  36.3 89.3 all-gather.4
  127.9 89.5 all-gather.2
  294.1 94.1 reduce-scatter.1
  402.2 84.0 all-reduce.4
where the time goes:
time: 507 us; the launch traced here: 502 us
  waiting for transfers between devices  297 us (59%)
  matrix products  120 us (24%)
  blocking collectives  34.1 us (7%)
  local copies, waits for them, and re-layouts  22.7 us (4%)
  between operations  14.4 us (3%)
  other arithmetic  8.74 us (2%)
  starting transfers between devices  5.36 us (1%)
    dot_general x20, matrix products, contract_pair(): lax.dot_general(left, right, (((left_axis,), (right_axis,)), ((), ())), p...  120 us
    psum x1, waiting for transfers between devices, local(): lax.psum(shared_slice[0].astype(jnp.bfloat16), 'dp').astype(jnp.float32)  80.9 us
    reduce_scatter x1, waiting for transfers between devices, local(): lax.psum_scatter(rows_part.astype(jnp.bfloat16), 'dp', scatter_dimension=...  78.8 us
    all_gather x1, waiting for transfers between devices, local(): lax.all_gather(recv_dy[0], 'dp', axis=0, tiled=True)  73.6 us
    all_gather x1, waiting for transfers between devices, local(): lax.all_gather(recv_x[0], 'dp', axis=0, tiled=True)  63.9 us
    all_to_all x1, blocking collectives, local(): lax.all_to_all(send_x, 'expert', split_axis=0, concat_axis=2, tiled=True)  18.4 us
    all_to_all x1, blocking collectives, local(): lax.all_to_all(send_dy, 'expert', split_axis=0, concat_axis=2, tiled=True)  15.7 us
  transfers between devices with their start and end apart: 5, of which 4 were waited for; matrix products, arithmetic and copies ran while one was open for 12% of the time, Pallas kernels for 0%

commit v1 on v0

--- a/solution.py
+++ b/solution.py
@@ -1,9 +1,41 @@
+import functools
 import jax
 import jax.numpy as jnp
 from jax import lax
 from jax.sharding import PartitionSpec as P
 
 ADAPTER_SCALE = 2.0
+
+
+def _draw_runs(shard_in, axis_tag):
+    piece_out, v_now, t_next = (
+        lax.axis_size(axis_tag),
+        lax.axis_index(axis_tag),
+        shard_in.shape[0],
+    )
+    leaves = tuple((h * piece_out if pp == 0 else h for pp, h in enumerate(shard_in.shape)))
+    found_now = lax.dynamic_update_slice_in_dim(
+        jnp.zeros(leaves, shard_in.dtype), shard_in, v_now * t_next, axis=0
+    )
+    x_new = d_next = shard_in
+    for s in tuple(range(1, piece_out // 2 + 1)):
+        x_new = lax.ppermute(
+            x_new, axis_tag, tuple(((pp, (pp + 1) % piece_out) for pp in range(piece_out)))
+        )
+        found_now = lax.dynamic_update_slice_in_dim(
+            found_now, x_new, (v_now - s) % piece_out * t_next, axis=0
+        )
+        if 2 * s < piece_out:
+            d_next = lax.ppermute(
+                d_next, axis_tag, tuple(((pp, (pp - 1) % piece_out) for pp in range(piece_out)))
+            )
+            found_now = lax.dynamic_update_slice_in_dim(
+                found_now, d_next, (v_now + s) % piece_out * t_next, axis=0
+            )
+    return found_now
+
+
+try_all_slot_here = functools.partial(_draw_runs, axis_tag="dp")
 
 
 def contract_pair(left, right, left_axis, right_axis):
@@ -156,9 +188,7 @@
         lax.all_to_all(send_dy, "expert", split_axis=0, concat_axis=2, tiled=True),
     )
     gradient_rows_out, shared_slice, owned_slice = rows_backward_pass(
-        lax.all_gather(recv_x[0], "dp", axis=0, tiled=True),
-        lax.all_gather(recv_dy[0], "dp", axis=0, tiled=True),
-        params,
+        try_all_slot_here(recv_x[0]), lax.all_gather(recv_dy[0], "dp", axis=0, tiled=True), params
     )
     rows_part = gradient_rows_out
     totals = (

time: 507 us -> 591 us (1.17)
  starting transfers between devices: 5.36 us -> 43.7 us
  local copies, waits for them, and re-layouts: 22.7 us -> 43.8 us
  waiting for transfers between devices: 297 us -> 310 us
  matrix products: 120 us -> 126 us
    ppermute x0 -> x15, waiting for transfers between devices: none -> 153 us  [the longest x7 121 us: _draw_runs(): lax.ppermute(d_next, axis_tag, tuple(((pp, (pp - 1) % piece_out) for pp i...]
    all_gather x1, waiting for transfers between devices: 73.6 us -> 0.01 us  [local(): lax.all_gather(recv_dy[0], 'dp', axis=0, tiled=True)]
    all_gather x1 -> x0, waiting for transfers between devices: 63.9 us -> none  [local(): lax.all_gather(recv_x[0], 'dp', axis=0, tiled=True)]
    ppermute x0 -> x15, starting transfers between devices: none -> 38.9 us  [the longest x7 38.5 us: _draw_runs(): lax.ppermute(d_next, axis_tag, tuple(((pp, (pp - 1) % piece_out) for pp i...]
    dynamic_update_slice x0 -> x16, local copies, waits for them, and re-layouts: none -> 15.3 us  [the longest x8 7.59 us: _draw_runs(): lax.dynamic_update_slice_in_dim(found_now, x_new, (v_now - s) % piece_out...]
    dot_general x20, matrix products: 120 us -> 126 us  [contract_pair(): lax.dot_general(left, right, (((left_axis,), (right_axis,)), ((), ())), p...]
    broadcast_in_dim x0 -> x1, local copies, waits for them, and re-layouts: none -> 6.11 us  [_draw_runs(): jnp.zeros(leaves, shard_in.dtype)]
  transfers between devices with their start and end apart: 5 -> 19, of which waited for: 4 -> 10; matrix products, arithmetic and copies ran while one was open for 12% -> 13% of each run, Pallas kernels for 0% -> 0%
where the time goes in v1:
time: 591 us; the launch traced here: 581 us
  waiting for transfers between devices  310 us (52%)
  matrix products  126 us (21%)
  local copies, waits for them, and re-layouts  43.8 us (7%)
  starting transfers between devices  43.7 us (7%)
  blocking collectives  34.1 us (6%)
  between operations  14.5 us (2%)
  other arithmetic  8.75 us (1%)
    dot_general x20, matrix products, contract_pair(): lax.dot_general(left, right, (((left_axis,), (right_axis,)), ((), ())), p...  126 us
    ppermute x7, waiting for transfers between devices, _draw_runs(): lax.ppermute(d_next, axis_tag, tuple(((pp, (pp - 1) % piece_out) for pp i...  121 us
    psum x1, waiting for transfers between devices, local(): lax.psum(shared_slice[0].astype(jnp.bfloat16), 'dp').astype(jnp.float32)  79.6 us
    reduce_scatter x1, waiting for transfers between devices, local(): lax.psum_scatter(rows_part.astype(jnp.bfloat16), 'dp', scatter_dimension=...  77.3 us
    ppermute x7, starting transfers between devices, _draw_runs(): lax.ppermute(d_next, axis_tag, tuple(((pp, (pp - 1) % piece_out) for pp i...  38.5 us
    ppermute x8, waiting for transfers between devices, _draw_runs(): lax.ppermute(x_new, axis_tag, tuple(((pp, (pp + 1) % piece_out) for pp in...  32.4 us
    all_to_all x1, blocking collectives, local(): lax.all_to_all(send_dy, 'expert', split_axis=0, concat_axis=2, tiled=True)  18.4 us
    all_to_all x1, blocking collectives, local(): lax.all_to_all(send_x, 'expert', split_axis=0, concat_axis=2, tiled=True)  15.7 us
  transfers between devices with their start and end apart: 19, of which 10 were waited for; matrix products, arithmetic and copies ran while one was open for 13% of the time, Pallas kernels for 0%

profile of v1, /device:TPU:0, one launch (start us, length us, event | category | flops | bytes accessed | tf_op | source)
XLA Modules:
  0.0 581.0 jit_solution(491482461115987259)
XLA Ops:
  22.1 18.4 %all_to_all.35 = bf16[8,96,512]{2,1,0:T(8,128)(2,1)S(1)} all-to-all(bf16[8,96,512]{2,1,0:T(8,128)(2,1)S(1)} %fusion.31), channel_id=1, replica_groups=mesh['dp'=16,'expert'=8] {'expert'}, dimensions={0} | all-to-all | bytes 1572864 | tf_op jit(solution)/shard_map/all_to_all | solution.py:188
  44.3 15.7 %all_to_all.36 = bf16[8,96,512]{2,1,0:T(8,128)(2,1)S(1)} all-to-all(bf16[8,96,512]{2,1,0:T(8,128)(2,1)S(1)} %bitcast.126), channel_id=1, replica_groups=mesh['dp'=16,'expert'=8] {'expert'}, dimensions={0} | all-to-all | bytes 1572864 | tf_op jit(solution)/shard_map/all_to_all | solution.py:187
  65.3 6.1 %broadcast_in_dim.58 = bf16[1536,4096]{1,0:T(8,128)(2,1)} broadcast(bf16[]{:T(256)} %constant.123.clone.1), dimensions={} | broadcast | bytes 12582914 | tf_op jit(solution)/shard_map/broadcast_in_dim | solution.py:18
  72.5 12.2 %collective-permute-done.1 = bf16[96,4096]{1,0:T(8,128)(2,1)S(1)} collective-permute-done((bf16[96,4096]{1,0:T(8,128)(2,1)S(1)}, bf16[96,4096]{1,0:T(8,128)(2,1)S(1)}, u32[]{:S(2)}, u32[]{:S(2)}) %collective-permute-start.1) | collective-permute-done | bytes 786464 | tf_op jit(solution)/shard_map/ppermute | solution.py:29
  90.8 28.0 %collective-permute-done.3 = bf16[96,4096]{1,0:T(8,128)(2,1)S(1)} collective-permute-done((bf16[96,4096]{1,0:T(8,128)(2,1)S(1)}, bf16[96,4096]{1,0:T(8,128)(2,1)S(1)}, u32[]{:S(2)}, u32[]{:S(2)}) %collective-permute-start.3) | collective-permute-done | bytes 786464 | tf_op jit(solution)/shard_map/ppermute | solution.py:29
  126.4 31.0 %collective-permute-done.5 = bf16[96,4096]{1,0:T(8,128)(2,1)S(1)} collective-permute-done((bf16[96,4096]{1,0:T(8,128)(2,1)S(1)}, bf16[96,4096]{1,0:T(8,128)(2,1)S(1)}, u32[]{:S(2)}, u32[]{:S(2)}) %collective-permute-start.5) | collective-permute-done | bytes 786464 | tf_op jit(solution)/shard_map/ppermute | solution.py:29
  165.2 24.4 %collective-permute-done.7 = bf16[96,4096]{1,0:T(8,128)(2,1)S(1)} collective-permute-done((bf16[96,4096]{1,0:T(8,128)(2,1)S(1)}, bf16[96,4096]{1,0:T(8,128)(2,1)S(1)}, u32[]{:S(2)}, u32[]{:S(2)}) %collective-permute-start.7) | collective-permute-done | bytes 786464 | tf_op jit(solution)/shard_map/ppermute | solution.py:29
  197.3 13.0 %collective-permute-done.9 = bf16[96,4096]{1,0:T(8,128)(2,1)S(1)} collective-permute-done((bf16[96,4096]{1,0:T(8,128)(2,1)S(1)}, bf16[96,4096]{1,0:T(8,128)(2,1)S(1)}, u32[]{:S(2)}, u32[]{:S(2)}) %collective-permute-start.9) | collective-permute-done | bytes 786464 | tf_op jit(solution)/shard_map/ppermute | solution.py:29
  218.1 12.0 %collective-permute-done.11 = bf16[96,4096]{1,0:T(8,128)(2,1)S(1)} collective-permute-done((bf16[96,4096]{1,0:T(8,128)(2,1)S(1)}, bf16[96,4096]{1,0:T(8,128)(2,1)S(1)}, u32[]{:S(2)}, u32[]{:S(2)}) %collective-permute-start.11) | collective-permute-done | bytes 786464 | tf_op jit(solution)/shard_map/ppermute | solution.py:29
  237.7 16.7 %collective-permute-done.12 = bf16[96,4096]{1,0:T(8,128)(2,1)S(1)} collective-permute-done((bf16[96,4096]{1,0:T(8,128)(2,1)S(1)}, bf16[96,4096]{1,0:T(8,128)(2,1)S(1)}, u32[]{:S(2)}, u32[]{:S(2)}) %collective-permute-start.12) | collective-permute-done | bytes 786464 | tf_op jit(solution)/shard_map/ppermute | solution.py:22
  256.6 15.7 %collective-permute-done.14 = bf16[96,4096]{1,0:T(8,128)(2,1)S(1)} collective-permute-done((bf16[96,4096]{1,0:T(8,128)(2,1)S(1)}, bf16[96,4096]{1,0:T(8,128)(2,1)S(1)}, u32[]{:S(2)}, u32[]{:S(2)}) %collective-permute-start.14) | collective-permute-done | bytes 786464 | tf_op jit(solution)/shard_map/ppermute | solution.py:22
  273.3 8.1 %convolution_convert_fusion.4 = bf16[1536,16]{0,1:T(8,128)(2,1)S(1)} fusion(bf16[1536,4096]{1,0:T(8,128)(2,1)} %constant_dynamic-update-slice_fusion, bf16[1,16,4096]{2,1,0:T(8,128)(2,1)S(1)} %copy-done.5), kind=kOutput, calls=%fused_computation.44 | convolution fusion | flops 201351168 | bytes 12763136 | tf_op jit(solution)/shard_map/dot_general | solution.py:42
  287.5 7.4 %fusion.23 = f32[448,1536]{1,0:T(8,128)} fusion(f32[1536,448]{0,1:T(8,128)S(1)} %convolution_multiply_fusion.3, bf16[1536,4096]{1,0:T(8,128)(2,1)S(1)} %copy-done.2, bf16[1,448,4096]{2,1,0:T(8,128)(2,1)S(1)} %copy-done.12), kind=kOutput, calls=%fused_computation.32 | convolution fusion | flops 5637832704 | bytes 21757952 | tf_op jit(solution)/shard_map/dot_general | solution.py:42
  294.9 8.2 %convolution_convert_fusion.5 = bf16[1536,16]{0,1:T(8,128)(2,1)S(1)} fusion(bf16[1536,4096]{1,0:T(8,128)(2,1)} %all-gather.2.cloned.1.call-done, bf16[1,4096,16]{1,2,0:T(8,128)(2,1)S(1)} %copy-done), kind=kOutput, calls=%fused_computation.45 | convolution fusion | flops 201351168 | bytes 12763136 | tf_op jit(solution)/shard_map/dot_general | solution.py:42
  303.2 9.3 %fusion.14 = f32[1536,448]{0,1:T(8,128)S(1)} fusion(bf16[1536,4096]{1,0:T(8,128)(2,1)} %all-gather.2.cloned.1.call-done, bf16[1,448,4096]{2,1,0:T(8,128)(2,1)S(1)} %copy-done.11), kind=kOutput, calls=%fused_computation.24 | convolution fusion | flops 5637144576 | bytes 19005440 | tf_op jit(solution)/shard_map/dot_general | solution.py:42
  314.3 12.0 %multiply_convert_fusion = (bf16[448,1536]{1,0:T(8,128)(2,1)}, bf16[448,1536]{1,0:T(8,128)(2,1)S(1)}, bf16[448,1536]{1,0:T(8,128)(2,1)S(1)}) fusion(f32[448,1536]{1,0:T(8,128)} %fusion.23, f32[448,1536]{1,0:T(8,128)S(1)} %fusion.29, f32[1536,448]{0,1:T(8,128)S(1)} %copy-done.3, bf16[1536,4096]{1,0:T(8,128)(2,1)S(1)} %bitcast.123, ...), kind=kOutput, calls=%fused_computation.35 | convolution fusion | flops 5648154624 | bytes 28639232 | tf_op jit(solution)/shard_map/dot_general | solution.py:42
  326.6 13.9 %fusion.10 = f32[1536,4096]{1,0:T(8,128)} fusion(bf16[448,1536]{1,0:T(8,128)(2,1)S(1)} %get-tuple-element.12, bf16[1,448,4096]{2,1,0:T(8,128)(2,1)} %param.18), kind=kOutput, calls=%fused_computation.20 | convolution fusion | flops 5637144576 | bytes 30212096 | tf_op jit(solution)/shard_map/dot_general | solution.py:42
  340.8 12.0 %fusion.6 = f32[1536,4096]{1,0:T(8,128)} fusion(bf16[448,1536]{1,0:T(8,128)(2,1)S(1)} %get-tuple-element.11, bf16[1,448,4096]{2,1,0:T(8,128)(2,1)S(1)} %copy-done.13), kind=kOutput, calls=%fused_computation.16 | convolution fusion | flops 5637144576 | bytes 30212096 | tf_op jit(solution)/shard_map/dot_general | solution.py:42
  352.7 21.9 %add_convert_fusion = bf16[1536,4096]{1,0:T(8,128)(2,1)} fusion(f32[1536,4096]{1,0:T(8,128)} %fusion.6, f32[1536,4096]{1,0:T(8,128)} %fusion.10, bf16[16,4096]{1,0:T(8,128)(2,1)S(1)} %bitcast.138, bf16[16,4096]{1,0:T(8,128)(2,1)S(1)} %bitcast.137, bf16[16,1536]{1,0:T(8,128)(2,1)S(1)} %bitcast.136, bf16[16,1536]{1,0:T(8,128)(2,1)S(1)} %bitcast.135), kind=kOutput, calls=%fused_computation.6 | convolution fusion | flops 428539904 | bytes 63275008 | tf_op jit(solution)/shard_map/dot_general | solution.py:42
  374.9 7.0 %fusion.4 = bf16[1,16,4096]{2,1,0:T(8,128)(2,1)} fusion(bf16[1536,16]{0,1:T(8,128)(2,1)S(1)} %convolution_convert_fusion.1, bf16[1536,4096]{1,0:T(8,128)(2,1)} %constant_dynamic-update-slice_fusion), kind=kOutput, calls=%fused_computation.14 | convolution fusion | flops 201457664 | bytes 12763136 | tf_op jit(solution)/shard_map/dot_general | solution.py:42
  381.9 7.6 %fusion.3 = bf16[1,4096,16]{1,2,0:T(8,128)(2,1)} fusion(bf16[1536,4096]{1,0:T(8,128)(2,1)} %all-gather.2.cloned.1.call-done, bf16[448,1536]{1,0:T(8,128)(2,1)} %get-tuple-element.10, bf16[1,16,448]{2,1,0:T(8,128)(2,1)S(1)} %copy-done.10), kind=kOutput, calls=%fused_computation.13 | convolution fusion | flops 223502336 | bytes 14104576 | tf_op jit(solution)/shard_map/dot_general | solution.py:42
  389.5 77.3 %reduce-scatter.2.cloned.1.call-done = bf16[96,4096]{1,0:T(8,128)(2,1)} async-done(((bf16[1536,4096]{1,0:T(8,128)(2,1)}), bf16[96,4096]{1,0:T(8,128)(2,1)}) %reduce-scatter.2.cloned.1.call-update) | async-done | bytes 786448 | tf_op jit(solution)/shard_map/reduce_scatter | solution.py:200
  473.6 7.0 %fusion.5 = bf16[1,16,4096]{2,1,0:T(8,128)(2,1)} fusion(bf16[1536,16]{0,1:T(8,128)(2,1)S(1)} %convolution_convert_fusion.2, bf16[1536,4096]{1,0:T(8,128)(2,1)} %constant_dynamic-update-slice_fusion), kind=kOutput, calls=%fused_computation.15 | convolution fusion | flops 201457664 | bytes 12763136 | tf_op jit(solution)/shard_map/dot_general | solution.py:42
  485.3 79.6 %all-reduce.5.cloned.1.call-done = (bf16[1,16,4096]{2,1,0:T(8,128)(2,1)}, bf16[1,16,4096]{2,1,0:T(8,128)(2,1)}, bf16[1,4096,16]{1,2,0:T(8,128)(2,1)}) async-done(((bf16[1,16,4096]{2,1,0:T(8,128)(2,1)}, bf16[1,16,4096]{2,1,0:T(8,128)(2,1)}, bf16[1,4096,16]{1,2,0:T(8,128)(2,1)}), (bf16[1,16,4096]{2,1,0:T(8,128)(2,1)}, bf16[1,16,4096]{2,1,0:T(8,128)(2,1)}, ...) | async-done | bytes 393232 | tf_op jit(solution)/shard_map/psum | solution.py:215
  (132 shorter events, 102.1 us)
Async XLA Ops:
  7.2 287.8 %copy-start = (bf16[1,4096,16]{1,2,0:T(8,128)(2,1)S(1)}, bf16[1,4096,16]{1,2,0:T(8,128)(2,1)}, u32[]{:S(2)}) copy-start(bf16[1,4096,16]{1,2,0:T(8,128)(2,1)} %param.25) | copy-start | bytes 393220
  7.2 287.7 %all-gather.2.cloned.1.call-start = ((), (), s32[]{:S(2)}) async-start(), calls=%async_computation.4 | async-start | bytes 13369344 | tf_op jit(solution)/shard_map/all_gather | solution.py:191
  21.8 19.8 %copy-start.7 = (bf16[128,512]{1,0:T(8,128)(2,1)S(1)}, bf16[128,512]{1,0:T(8,128)(2,1)}, u32[]{:S(2)}) copy-start(bf16[128,512]{1,0:T(8,128)(2,1)} %param.13) | copy-start | bytes 393220
  41.5 425.2 %reduce-scatter.2.cloned.1.call-start = ((), (), s32[]{:S(2)}) async-start(), calls=%async_computation.5 | async-start | bytes 13369344 | tf_op jit(solution)/shard_map/reduce_scatter | solution.py:200
  60.1 24.6 %collective-permute-start.1 = (bf16[96,4096]{1,0:T(8,128)(2,1)S(1)}, bf16[96,4096]{1,0:T(8,128)(2,1)S(1)}, u32[]{:S(2)}, u32[]{:S(2)}) collective-permute-start(bf16[96,4096]{1,0:T(8,128)(2,1)S(1)} %bitcast.128), channel_id=1, source_target_pairs={{0,120},{8,0},{16,8},{24,16},{32,24},{40,32},{48,40},{56,48},{64,5... | collective-permute-start | bytes 2359304 | tf_op jit(solution)/shard_map/ppermute | solution.py:29
  65.3 23.5 %collective-permute-start = (bf16[96,4096]{1,0:T(8,128)(2,1)S(1)}, bf16[96,4096]{1,0:T(8,128)(2,1)S(1)}, u32[]{:S(2)}, u32[]{:S(2)}) collective-permute-start(bf16[96,4096]{1,0:T(8,128)(2,1)S(1)} %bitcast.129), channel_id=1, source_target_pairs={{0,8},{8,16},{16,24},{24,32},{32,40},{40,48},{48,56},{56,64},{64,7... | collective-permute-start | bytes 2359304 | tf_op jit(solution)/shard_map/ppermute | solution.py:22
  84.7 34.1 %collective-permute-start.3 = (bf16[96,4096]{1,0:T(8,128)(2,1)S(1)}, bf16[96,4096]{1,0:T(8,128)(2,1)S(1)}, u32[]{:S(2)}, u32[]{:S(2)}) collective-permute-start(bf16[96,4096]{1,0:T(8,128)(2,1)S(1)} %collective-permute-done.1), channel_id=1, source_target_pairs={{0,120},{8,0},{16,8},{24,16},{32,24},{40,32},{48,40},{56,48},{64,5... | collective-permute-start | bytes 2359304 | tf_op jit(solution)/shard_map/ppermute | solution.py:29
  88.9 35.7 %collective-permute-start.2 = (bf16[96,4096]{1,0:T(8,128)(2,1)S(1)}, bf16[96,4096]{1,0:T(8,128)(2,1)S(1)}, u32[]{:S(2)}, u32[]{:S(2)}) collective-permute-start(bf16[96,4096]{1,0:T(8,128)(2,1)S(1)} %collective-permute-done), channel_id=1, source_target_pairs={{0,8},{8,16},{16,24},{24,32},{32,40},{40,48},{48,56},{56,64},{64,7... | collective-permute-start | bytes 2359304 | tf_op jit(solution)/shard_map/ppermute | solution.py:22
  118.8 38.7 %collective-permute-start.5 = (bf16[96,4096]{1,0:T(8,128)(2,1)S(1)}, bf16[96,4096]{1,0:T(8,128)(2,1)S(1)}, u32[]{:S(2)}, u32[]{:S(2)}) collective-permute-start(bf16[96,4096]{1,0:T(8,128)(2,1)S(1)} %collective-permute-done.3), channel_id=1, source_target_pairs={{0,120},{8,0},{16,8},{24,16},{32,24},{40,32},{48,40},{56,48},{64,5... | collective-permute-start | bytes 2359304 | tf_op jit(solution)/shard_map/ppermute | solution.py:29
  124.6 38.7 %collective-permute-start.4 = (bf16[96,4096]{1,0:T(8,128)(2,1)S(1)}, bf16[96,4096]{1,0:T(8,128)(2,1)S(1)}, u32[]{:S(2)}, u32[]{:S(2)}) collective-permute-start(bf16[96,4096]{1,0:T(8,128)(2,1)S(1)} %collective-permute-done.2), channel_id=1, source_target_pairs={{0,8},{8,16},{16,24},{24,32},{32,40},{40,48},{48,56},{56,64},{64,7... | collective-permute-start | bytes 2359304 | tf_op jit(solution)/shard_map/ppermute | solution.py:22
  157.4 32.1 %collective-permute-start.7 = (bf16[96,4096]{1,0:T(8,128)(2,1)S(1)}, bf16[96,4096]{1,0:T(8,128)(2,1)S(1)}, u32[]{:S(2)}, u32[]{:S(2)}) collective-permute-start(bf16[96,4096]{1,0:T(8,128)(2,1)S(1)} %collective-permute-done.5), channel_id=1, source_target_pairs={{0,120},{8,0},{16,8},{24,16},{32,24},{40,32},{48,40},{56,48},{64,5... | collective-permute-start | bytes 2359304 | tf_op jit(solution)/shard_map/ppermute | solution.py:29
  163.2 32.2 %collective-permute-start.6 = (bf16[96,4096]{1,0:T(8,128)(2,1)S(1)}, bf16[96,4096]{1,0:T(8,128)(2,1)S(1)}, u32[]{:S(2)}, u32[]{:S(2)}) collective-permute-start(bf16[96,4096]{1,0:T(8,128)(2,1)S(1)} %collective-permute-done.4), channel_id=1, source_target_pairs={{0,8},{8,16},{16,24},{24,32},{32,40},{40,48},{48,56},{56,64},{64,7... | collective-permute-start | bytes 2359304 | tf_op jit(solution)/shard_map/ppermute | solution.py:22
  189.6 20.7 %collective-permute-start.9 = (bf16[96,4096]{1,0:T(8,128)(2,1)S(1)}, bf16[96,4096]{1,0:T(8,128)(2,1)S(1)}, u32[]{:S(2)}, u32[]{:S(2)}) collective-permute-start(bf16[96,4096]{1,0:T(8,128)(2,1)S(1)} %collective-permute-done.7), channel_id=1, source_target_pairs={{0,120},{8,0},{16,8},{24,16},{32,24},{40,32},{48,40},{56,48},{64,5... | collective-permute-start | bytes 2359304 | tf_op jit(solution)/shard_map/ppermute | solution.py:29
  195.4 20.7 %collective-permute-start.8 = (bf16[96,4096]{1,0:T(8,128)(2,1)S(1)}, bf16[96,4096]{1,0:T(8,128)(2,1)S(1)}, u32[]{:S(2)}, u32[]{:S(2)}) collective-permute-start(bf16[96,4096]{1,0:T(8,128)(2,1)S(1)} %collective-permute-done.6), channel_id=1, source_target_pairs={{0,8},{8,16},{16,24},{24,32},{32,40},{40,48},{48,56},{56,64},{64,7... | collective-permute-start | bytes 2359304 | tf_op jit(solution)/shard_map/ppermute | solution.py:22
  210.3 19.8 %collective-permute-start.11 = (bf16[96,4096]{1,0:T(8,128)(2,1)S(1)}, bf16[96,4096]{1,0:T(8,128)(2,1)S(1)}, u32[]{:S(2)}, u32[]{:S(2)}) collective-permute-start(bf16[96,4096]{1,0:T(8,128)(2,1)S(1)} %collective-permute-done.9), channel_id=1, source_target_pairs={{0,120},{8,0},{16,8},{24,16},{32,24},{40,32},{48,40},{56,48},{64,5... | collective-permute-start | bytes 2359304 | tf_op jit(solution)/shard_map/ppermute | solution.py:29
  216.1 19.8 %collective-permute-start.10 = (bf16[96,4096]{1,0:T(8,128)(2,1)S(1)}, bf16[96,4096]{1,0:T(8,128)(2,1)S(1)}, u32[]{:S(2)}, u32[]{:S(2)}) collective-permute-start(bf16[96,4096]{1,0:T(8,128)(2,1)S(1)} %collective-permute-done.8), channel_id=1, source_target_pairs={{0,8},{8,16},{16,24},{24,32},{32,40},{40,48},{48,56},{56,64},{64,7... | collective-permute-start | bytes 2359304 | tf_op jit(solution)/shard_map/ppermute | solution.py:22
  218.1 55.2 %copy-start.5 = (bf16[1,16,4096]{2,1,0:T(8,128)(2,1)S(1)}, bf16[1,16,4096]{2,1,0:T(8,128)(2,1)}, u32[]{:S(2)}) copy-start(bf16[1,16,4096]{2,1,0:T(8,128)(2,1)} %param.22) | copy-start | bytes 393220
  230.0 25.7 %collective-permute-start.13 = (bf16[96,4096]{1,0:T(8,128)(2,1)S(1)}, bf16[96,4096]{1,0:T(8,128)(2,1)S(1)}, u32[]{:S(2)}, u32[]{:S(2)}) collective-permute-start(bf16[96,4096]{1,0:T(8,128)(2,1)S(1)} %collective-permute-done.11), channel_id=1, source_target_pairs={{0,120},{8,0},{16,8},{24,16},{32,24},{40,32},{48,40},{56,48},{64,5... | collective-permute-start | bytes 2359304 | tf_op jit(solution)/shard_map/ppermute | solution.py:29
  235.8 18.6 %collective-permute-start.12 = (bf16[96,4096]{1,0:T(8,128)(2,1)S(1)}, bf16[96,4096]{1,0:T(8,128)(2,1)S(1)}, u32[]{:S(2)}, u32[]{:S(2)}) collective-permute-start(bf16[96,4096]{1,0:T(8,128)(2,1)S(1)} %collective-permute-done.10), channel_id=1, source_target_pairs={{0,8},{8,16},{16,24},{24,32},{32,40},{40,48},{48,56},{56,64},{64,7... | collective-permute-start | bytes 2359304 | tf_op jit(solution)/shard_map/ppermute | solution.py:22
  254.4 18.0 %collective-permute-start.14 = (bf16[96,4096]{1,0:T(8,128)(2,1)S(1)}, bf16[96,4096]{1,0:T(8,128)(2,1)S(1)}, u32[]{:S(2)}, u32[]{:S(2)}) collective-permute-start(bf16[96,4096]{1,0:T(8,128)(2,1)S(1)} %collective-permute-done.12), channel_id=1, source_target_pairs={{0,8},{8,16},{16,24},{24,32},{32,40},{40,48},{48,56},{56,64},{64,7... | collective-permute-start | bytes 2359304 | tf_op jit(solution)/shard_map/ppermute | solution.py:22
  294.9 18.2 %slice-start = ((s8[12582912]{0:T(1024)(128)(4,1)}), s8[4194304]{0:T(1024)(128)(4,1)S(1)}, s32[]{:S(2)}) async-start(s8[12582912]{0:T(1024)(128)(4,1)} %bitcast.122), calls=%async_computation.7 | async-start | bytes 8388608
  326.6 14.2 %copy-start.13 = (bf16[1,448,4096]{2,1,0:T(8,128)(2,1)S(1)}, bf16[1,448,4096]{2,1,0:T(8,128)(2,1)}, u32[]{:S(2)}) copy-start(bf16[1,448,4096]{2,1,0:T(8,128)(2,1)} %param.17) | copy-start | bytes 11010052
  468.9 100.9 %all-to-all-start.2 = ((bf16[96,8,512]{2,0,1:T(8,128)(2,1)}), bf16[96,8,512]{2,0,1:T(8,128)(2,1)}, u32[]{:S(2)}, u32[]{:S(2)}) async-start(bf16[96,8,512]{2,0,1:T(8,128)(2,1)} %bitcast.131), calls=%async_computation.3 | async-start | bytes 1572864 | tf_op jit(solution)/shard_map/all_to_all | solution.py:203
  473.3 91.6 %all-reduce.5.cloned.1.call-start = ((), (), s32[]{:S(2)}) async-start(), calls=%async_computation.6 | async-start | bytes 786432 | tf_op jit(solution)/shard_map/psum | solution.py:215
  (12 other events, 91.2 us)
Sparse Core Ops, SparseCore 0:
  41.7 149.6 all-gather.1
  374.7 92.0 reduce-scatter.1
  480.7 84.1 all-reduce.4
